TPU v7x, 32 devices: a whole 2x2x4 slice. The times are simulated.
32 devices in a mesh: ckpt: 8 (over y, x, core), vocab: 4 (over z).
Axes of the slice: x: 2, y: 2, z: 4, core: 2. Of those that a mesh axis runs over, the one named last changes fastest.
Arguments:
- hidden_rows: bfloat16 [8, 128, 768], P('ckpt'), may hold values from -8 to 8
- norm_gain: float32 [8, 768], P('ckpt'), may hold values from 0.5 to 1.5
- norm_bias: float32 [8, 768], P('ckpt'), may hold values from -1.2 to 1.2
- unembed: bfloat16 [8, 768, 50304], P('ckpt', None, 'vocab'), may hold values from -6 to 6
- target_ids: int32 [128], replicated, may hold values from 0 to 50303
- ckpt_steps: int32 [8], replicated, may hold values from 0 to 143000
- components: int32 [1], replicated, may hold values from 1 to 8
Outputs:
- loadings: bfloat16 [8, 128, 50304], P(None, 'ckpt', 'vocab')
- gram: float32 [8, 8], replicated
- target_logprob: float32 [8, 128], P('ckpt')
All inputs are finite; a program needn't handle non-finite values.
Results may differ from a plain program's by a relative error of at most 0.0063.
Values may be sent and summed in bfloat16 or wider, within the bound.
A program may use at most 192 MiB of HBM per device.

v0:
```python
import jax
import jax.numpy as jnp
from jax import lax
from jax.sharding import PartitionSpec as P

COMPONENTS = 8


def normalize_rows(rows, ids, weights, columns):
    logits = jnp.dot(rows, weights, preferred_element_type=jnp.float32)
    hits = columns[None, :] == ids[:, None]
    target_logit = jnp.sum(jnp.where(hits, logits, 0.0), axis=1)
    local_top = jnp.max(logits, axis=1)
    top = lax.pmax(local_top, "vocab")
    local_sum = jnp.sum(jnp.exp(logits - top[:, None]), axis=1)
    total, target_sum = lax.psum((local_sum, target_logit), "vocab")
    lse = top + jnp.log(total)
    logprob = (logits - lse[:, None]).astype(jnp.bfloat16)
    return (logprob, target_sum - lse)


def per_device(hidden_rows, norm_gain, norm_bias, unembed, target_ids, ckpt_steps, components):
    owners = lax.axis_size("ckpt")
    shards = lax.axis_size("vocab")
    width = unembed.shape[2]
    tokens = hidden_rows.shape[1]
    slab = tokens // owners
    columns = lax.axis_index("vocab") * width + jnp.arange(width, dtype=jnp.int32)
    floats = hidden_rows[0].astype(jnp.float32)
    centre = jnp.mean(floats, axis=1, keepdims=True)
    spread = jnp.mean((floats - centre) ** 2, axis=1, keepdims=True)
    normed = (
        (floats - centre) / jnp.sqrt(spread + 1e-05) * norm_gain[0][None, :] + norm_bias[0][None, :]
    ).astype(jnp.bfloat16)
    weights = unembed[0]
    blocks = 1
    part_rows = slab // blocks
    grouped = normed.reshape(owners, blocks, part_rows, normed.shape[1])
    grouped_ids = target_ids.reshape(owners, blocks, part_rows)
    rows = grouped[:, 0].reshape(owners * part_rows, normed.shape[1])
    ids = grouped_ids[:, 0].reshape(owners * part_rows)
    logprob, target_part = normalize_rows(rows, ids, weights, columns)
    outgoing = logprob.reshape(1, owners, part_rows, width)
    incoming = lax.all_to_all(outgoing, "ckpt", split_axis=1, concat_axis=0, tiled=True)
    received = incoming.reshape(owners, part_rows, width)
    targets = target_part.reshape(owners, part_rows)
    target_logprob = targets.reshape(1, tokens)
    values = received.astype(jnp.float32)
    centred = (values - jnp.mean(values, axis=0, keepdims=True)).reshape(owners, slab * width)
    partial_gram = jnp.dot(centred, centred.T, precision=lax.Precision.HIGHEST)
    gram = lax.psum(partial_gram, ("ckpt", "vocab")) / (tokens * width * shards)
    count = gram.shape[0]
    kinds = unembed.shape[0] * 0 + COMPONENTS
    freqs = jnp.arange(kinds).astype(jnp.float32) + 1.0
    basis = jnp.cos(jnp.pi * freqs[None, :] * ckpt_steps.astype(jnp.float32)[:, None] / 143000.0)
    trace = jnp.sum(jnp.diagonal(gram))
    mixing = jnp.dot(gram, basis, precision=lax.Precision.HIGHEST) / (trace / count + 1e-06)
    keep = (jnp.arange(kinds) < components[0]).astype(jnp.float32)
    mixed = jnp.dot(mixing.T, centred, precision=lax.Precision.HIGHEST) / count
    loadings = (mixed * keep[:, None]).reshape(kinds, slab, width).astype(jnp.bfloat16)
    return (loadings, gram, target_logprob)


def solution(mesh):
    return jax.shard_map(
        per_device,
        mesh=mesh,
        in_specs=(
            P("ckpt", None, None),
            P("ckpt", None),
            P("ckpt", None),
            P("ckpt", None, "vocab"),
            P(),
            P(),
            P(),
        ),
        out_specs=(P(None, "ckpt", "vocab"), P(), P("ckpt", None)),
        check_vma=False,
    )
```

profile of v0, /device:TPU:0, one launch (start us, length us, event | category | flops | bytes accessed | tf_op | source)
XLA Modules:
  0.0 187.3 jit_solution(2018327534467279010)
XLA Ops:
  0.6 1.0 convert_reduce_fusion.1
  1.7 1.1 fusion.16
  2.8 0.7 reduce.2
  3.5 0.7 reduce.3
  4.2 0.0 copy-start.1
  4.2 11.2 %fusion.30 = (f32[128]{0:T(128)S(1)}, f32[128,12576]{0,1:T(8,128)}) fusion(bf16[1,768,12576]{1,2,0:T(8,128)(2,1)} %param.10, bf16[1,128,768]{2,1,0:T(8,128)(2,1)} %param.7, f32[768]{0:T(1024)S(1)} %reduce.3, f32[768]{0:T(1024)S(1)} %reduce.2, f32[128]{0:T(128)S(1)} %add_sqrt_fusion, f32[128]{0:T(128)S(1)} %broadcast_multiply_fusion.2), kind=kOutput, calls=%fused_computation.48 | convolution fusion | flops 2474741760 | bytes 25959936 | tf_op jit(solution)/shard_map/dot_general | solution.py:10
  15.4 13.5 %pmax.7 = f32[128]{0:T(128)S(1)} all-reduce(f32[128]{0:T(128)S(1)} %get-tuple-element.9), channel_id=1, replica_groups=mesh['ckpt'=8,'vocab'=4] {'vocab'}, use_global_device_ids=true, to_apply=%region_3.4 | all-reduce | flops 128 | bytes 1024 | tf_op jit(solution)/shard_map/pmax | solution.py:14
  28.9 0.0 copy-done.1
  28.9 8.8 %select_reduce_fusion = (f32[128]{0:T(128)S(1)}, f32[128]{0:T(128)S(1)}) fusion(f32[128,12576]{0,1:T(8,128)} %get-tuple-element.10, s32[128]{0:T(128)S(1)} %copy-done.1, s32[12576]{0:T(1024)S(1)} %iota_add_fusion, f32[128]{0:T(128)S(1)} %pmax.7), kind=kLoop, calls=%fused_computation.8 | loop fusion | flops 8048384 | bytes 6491264 | tf_op jit(solution)/shard_map/reduce_sum | solution.py:12
  37.6 8.4 %all-reduce = (f32[128]{0:T(128)S(1)}, f32[128]{0:T(128)S(1)}) all-reduce(f32[128]{0:T(128)S(1)} %get-tuple-element.4, f32[128]{0:T(128)S(1)} %get-tuple-element.3), channel_id=1, replica_groups=mesh['ckpt'=8,'vocab'=4] {'vocab'}, use_global_device_ids=true, to_apply=%region_5.6 | all-reduce | flops 256 | bytes 2048 | tf_op jit(solution)/shard_map/psum | solution.py:16
  46.0 0.5 subtract_bitcast_fusion.1
  46.5 3.1 %subtract_convert_fusion = bf16[128,12576]{0,1:T(8,128)(2,1)S(1)} fusion(f32[128,12576]{0,1:T(8,128)} %get-tuple-element.10, f32[128]{0:T(128)S(1)} %get-tuple-element.8), kind=kLoop, calls=%fused_computation.10 | loop fusion | flops 3219456 | bytes 9658880 | tf_op jit(solution)/shard_map/convert_element_type | solution.py:18
  49.6 0.0 copy-start.2
  49.6 3.7 %copy.14 = bf16[128,12576]{1,0:T(8,128)(2,1)} copy(bf16[128,12576]{0,1:T(8,128)(2,1)S(1)} %subtract_convert_fusion) | data formatting | bytes 6438912 | tf_op jit(solution)/shard_map/convert_element_type | solution.py:18
  53.3 3.8 %all-to-all-start = ((bf16[1,8,16,12576]{3,2,0,1:T(8,128)(2,1)}), bf16[1,8,16,12576]{3,2,0,1:T(8,128)(2,1)S(1)}, u32[]{:S(2)}, u32[]{:S(2)}) async-start(bf16[1,8,16,12576]{3,2,0,1:T(8,128)(2,1)} %bitcast.37), calls=%async_computation | async-start | bytes 6488064 | tf_op jit(solution)/shard_map/all_to_all | solution.py:44
  57.2 0.0 copy-done.2
  57.9 38.1 %all-to-all-done = bf16[1,8,16,12576]{3,2,0,1:T(8,128)(2,1)S(1)} async-done(((bf16[1,8,16,12576]{3,2,0,1:T(8,128)(2,1)}), bf16[1,8,16,12576]{3,2,0,1:T(8,128)(2,1)S(1)}, u32[]{:S(2)}, u32[]{:S(2)}) %all-to-all-start) | async-done | bytes 3219488 | tf_op jit(solution)/shard_map/all_to_all | solution.py:44
  95.9 0.5 convert_reduce_fusion
  96.4 0.9 broadcast_multiply_fusion
  97.4 2.5 %div.59 = f32[201216]{0:T(1024)} reshape(f32[16,12576]{1,0:T(8,128)} %broadcast_multiply_fusion) | data formatting | bytes 1609728 | tf_op jit(solution)/shard_map/div | solution.py:49
  99.9 1.6 subtract_bitcast_fusion
  101.5 14.3 %fusion.7 = f32[8,8]{1,0:T(8,128)S(1)} fusion(f32[8,16,12576]{2,1,0:T(8,128)S(1)} %subtract_bitcast_fusion), kind=kOutput, calls=%fused_computation.15 | convolution fusion | flops 154533888 | bytes 6439168 | tf_op jit(solution)/shard_map/dot_general | solution.py:50
  115.8 39.9 %psum.22 = f32[8,8]{1,0:T(8,128)S(1)} all-reduce(f32[8,8]{1,0:T(8,128)S(1)} %fusion.7), channel_id=1, replica_groups=mesh['ckpt'=8,'vocab'=4] {'ckpt','vocab'}, use_global_device_ids=true, to_apply=%region_7.8 | all-reduce | flops 64 | bytes 512 | tf_op jit(solution)/shard_map/psum | solution.py:51
  155.6 0.0 copy-start
  155.6 0.6 gather_fusion
  156.3 0.6 reduce_sum.58
  157.5 0.2 convolution_divide_fusion
  157.8 6.4 %reshape.101 = f32[8,201216]{1,0:T(8,128)} reshape(bf16[1,8,16,12576]{3,2,0,1:T(8,128)(2,1)S(1)} %all-to-all-done) | data formatting | bytes 9658368 | tf_op jit(solution)/shard_map/convert_element_type | solution.py:48
  164.2 9.6 %fusion = bf16[8,201216]{1,0:T(8,128)(2,1)S(1)} fusion(f32[8,8]{1,0:T(8,128)S(1)} %convolution_divide_fusion, f32[8,201216]{1,0:T(8,128)} %reshape.101, f32[8]{0:T(128)S(1)} %compare_select_fusion, f32[201216]{0:T(1024)} %div.59), kind=kOutput, calls=%fused_computation.2 | convolution fusion | flops 159363072 | bytes 10463520 | tf_op jit(solution)/shard_map/dot_general | solution.py:59
  173.8 0.0 copy-done
  173.8 6.5 %reshape.111 = bf16[1609728]{0:T(1024)(128)(2,1)} reshape(bf16[8,201216]{1,0:T(8,128)(2,1)S(1)} %fusion) | data formatting | bytes 6438912
  180.3 7.0 %convert_element_type.65 = bf16[8,16,12576]{2,1,0:T(8,128)(2,1)} reshape(bf16[1609728]{0:T(1024)(128)(2,1)} %reshape.111) | data formatting | bytes 6438912 | tf_op jit(solution)/shard_map/convert_element_type | solution.py:60
  (8 shorter events, 0.0 us)
Async XLA Ops:
  4.2 24.6 %copy-start.1 = (s32[128]{0:T(128)S(1)}, s32[128]{0:T(128)}, u32[]{:S(2)}) copy-start(s32[128]{0:T(128)} %param.11) | copy-start | bytes 1540
  49.6 7.5 %copy-start.2 = (s32[8]{0:T(128)S(1)}, s32[8]{0:T(128)}, u32[]{:S(2)}) copy-start(s32[8]{0:T(128)} %param.12) | copy-start | bytes 100
  53.3 42.6 %all-to-all-start = ((bf16[1,8,16,12576]{3,2,0,1:T(8,128)(2,1)}), bf16[1,8,16,12576]{3,2,0,1:T(8,128)(2,1)S(1)}, u32[]{:S(2)}, u32[]{:S(2)}) async-start(bf16[1,8,16,12576]{3,2,0,1:T(8,128)(2,1)} %bitcast.37), calls=%async_computation | async-start | bytes 6488064 | tf_op jit(solution)/shard_map/all_to_all | solution.py:44
  155.6 18.1 %copy-start = (f32[8,8]{1,0:T(8,128)}, f32[8,8]{1,0:T(8,128)S(1)}, u32[]{:S(2)}) copy-start(f32[8,8]{1,0:T(8,128)S(1)} %broadcast_multiply_fusion.1) | copy-start | bytes 772
where the time goes:
time: 188 us; the launch traced here: 187 us
  blocking collectives  61.7 us (33%)
  waiting for transfers between devices  38.1 us (20%)
  matrix products  35.3 us (19%)
  local copies, waits for them, and re-layouts  26.8 us (14%)
  other arithmetic  19.5 us (10%)
  starting transfers between devices  3.84 us (2%)
  between operations  2.06 us (1%)
    psum x1, blocking collectives, per_device(): gram = lax.psum(partial_gram, ('ckpt', 'vocab')) / (tokens * width * shards)  39.9 us
    all_to_all x1, waiting for transfers between devices, per_device(): lax.all_to_all(outgoing, 'ckpt', split_axis=1, concat_axis=0, tiled=True)  38.1 us
    dot_general x1, matrix products, per_device(): partial_gram = jnp.dot(centred, centred.T, precision=lax.Precision.HIGHEST)  14.3 us
    pmax x1, blocking collectives, normalize_rows(): top = lax.pmax(local_top, 'vocab')  13.5 us
    dot_general x1, matrix products, normalize_rows(): logits = jnp.dot(rows, weights, preferred_element_type=jnp.float32)  11.2 us
    dot_general x1, matrix products, per_device(): mixed = jnp.dot(mixing.T, centred, precision=lax.Precision.HIGHEST) / count  9.58 us
    reduce_sum x1, other arithmetic, normalize_rows(): target_logit = jnp.sum(jnp.where(hits, logits, 0.0), axis=1)  8.76 us
    psum x1, blocking collectives, normalize_rows(): total, target_sum = lax.psum((local_sum, target_logit), 'vocab')  8.37 us
  transfers between devices with their start and end apart: 1, of which 1 were waited for; matrix products, arithmetic and copies ran while one was open for 0% of the time, Pallas kernels for 0%

commit v1 on v0

v1 whole, which is shorter than its diff:
```python
import functools

import jax
import jax.numpy as jnp
from jax import lax
from jax.experimental import pallas as pl
from jax.experimental.pallas import tpu as pltpu
from jax.sharding import PartitionSpec as P

COMPONENTS = 8
LANES = 128
HIGH = lax.Precision.HIGHEST
MESH = pl.DeviceIdType.MESH
LOW = -1e30
NT = (((1,), (1,)), ((), ()))


def split_tiles(width):
    tiles = -(-width // LANES)
    best = tiles
    for per in range(1, tiles + 1):
        if tiles % per == 0 and per >= 6:
            best = per
            break
    return best * LANES, tiles // best


def spread_steps(steps_ref, shape, slab):
    lane_owner = lax.broadcasted_iota(jnp.int32, shape, 1) // slab
    out = jnp.zeros(shape, jnp.float32)
    for c in range(steps_ref.shape[0]):
        out = jnp.where(lane_owner == c, steps_ref[c].astype(jnp.float32), out)
    return out


def gather_kernel(
    sizes,
    hidden_ref, gain_ref, bias_ref, ids_ref, steps_ref, comps_ref, w_ref,
    xout_ref, whi_ref, wlo_ref, shift_ref, gram_ref, target_ref,
    normed, xsend, xrecv, off, ids, tops, sums, hits, stat, stats, dsend, drecv,
    gsend, grecv, hsend, hrecv,
    send_sem, recv_sem, out_sem, ssend, srecv, dssem, drsem, gssem, grsem, hssem, hrsem,
):
    owners, shards, tokens, width, tile, chunks = sizes
    slab = tokens // owners
    rows = owners * slab
    kinds = COMPONENTS
    me = lax.axis_index("ckpt")
    mine = lax.axis_index("vocab")
    step = pl.program_id(0)
    groups = tile // LANES
    my_rows = pl.ds(pl.multiple_of(me * slab, slab), slab)

    def peer(r):
        return lax.rem(me + r, owners)

    def side(r):
        return lax.rem(mine + r, shards)

    @pl.when(step == 0)
    def _():
        barrier = pltpu.get_barrier_semaphore()
        for r in range(1, owners):
            pl.semaphore_signal(barrier, inc=1, device_id=(peer(r), mine), device_id_type=MESH)
        for r in range(1, shards):
            pl.semaphore_signal(barrier, inc=1, device_id=(me, side(r)), device_id_type=MESH)
        floats = hidden_ref[...].astype(jnp.float32)
        centre = jnp.mean(floats, axis=1, keepdims=True)
        spread = jnp.mean((floats - centre) ** 2, axis=1, keepdims=True)
        normed[...] = (
            (floats - centre) / jnp.sqrt(spread + 1e-05) * gain_ref[...] + bias_ref[...]
        ).astype(jnp.bfloat16)
        wide = jnp.broadcast_to(ids_ref[...].astype(jnp.float32), (LANES, tokens))
        ids[...] = jnp.transpose(wide).astype(jnp.int32)
        tops[...] = jnp.full_like(tops, LOW)
        sums[...] = jnp.zeros_like(sums)
        hits[...] = jnp.zeros_like(hits)

    logits = jnp.dot(normed[...], w_ref[...], preferred_element_type=jnp.float32)
    first = step * tile
    lane = lax.broadcasted_iota(jnp.int32, (tokens, LANES), 1)

    @pl.when(step == 0)
    def _():
        total = logits[:, :LANES]
        for g in range(1, groups):
            total = total + logits[:, g * LANES:(g + 1) * LANES]
        off[...] = jnp.broadcast_to(
            jnp.sum(total, axis=1, keepdims=True) * (1.0 / tile), off.shape
        )

    shift = off[...]
    for g in range(groups):
        part = logits[:, g * LANES:(g + 1) * LANES]
        inside = (first + g * LANES + lane) < width
        at = pl.multiple_of(first + g * LANES, LANES)
        xsend[:, pl.ds(at, LANES)] = jnp.where(inside, part - shift, 0.0).astype(jnp.bfloat16)

    @pl.when(step == 0)
    def _():
        barrier = pltpu.get_barrier_semaphore()
        pl.semaphore_wait(barrier, owners - 1 + shards - 1)

    def columns(j):
        return pl.ds(pl.multiple_of(j * tile, LANES), tile)

    for r in range(1, owners):
        to = peer(r)
        pltpu.make_async_remote_copy(
            src_ref=xsend.at[pl.ds(pl.multiple_of(to * slab, slab), slab), columns(step)],
            dst_ref=xrecv.at[my_rows, columns(step)],
            send_sem=send_sem.at[r],
            recv_sem=recv_sem.at[step],
            device_id=(to, mine),
            device_id_type=MESH,
        ).start()
    pltpu.make_async_copy(
        xsend.at[my_rows, columns(step)], xrecv.at[my_rows, columns(step)], recv_sem.at[step]
    ).start()

    old_top = tops[...]
    new_top = old_top
    parts = []
    for g in range(groups):
        part = logits[:, g * LANES:(g + 1) * LANES]
        inside = (first + g * LANES + lane) < width
        part = jnp.where(inside, part, LOW)
        parts.append(part)
        new_top = jnp.maximum(new_top, part)
    acc = sums[...] * jnp.exp(old_top - new_top)
    hit = hits[...]
    start = mine * width + first
    wanted = ids[...] - start
    for g in range(groups):
        acc = acc + jnp.exp(parts[g] - new_top)
        col = g * LANES + lane
        hit = hit + jnp.where((col == wanted) & ((first + col) < width), parts[g], 0.0)
    tops[...] = new_top
    sums[...] = acc
    hits[...] = hit

    @pl.when(step == chunks - 1)
    def _():
        top = jnp.max(tops[...], axis=1, keepdims=True)
        total = jnp.sum(sums[...] * jnp.exp(tops[...] - top), axis=1, keepdims=True)
        picked = jnp.sum(hits[...], axis=1, keepdims=True)
        stat[...] = jnp.where(lane == 0, top, jnp.where(lane == 1, total, picked))
        sent = []
        for r in range(1, shards):
            copy = pltpu.make_async_remote_copy(
                src_ref=stat,
                dst_ref=stats.at[r - 1],
                send_sem=ssend.at[r - 1],
                recv_sem=srecv.at[r - 1],
                device_id=(me, side(r)),
                device_id_type=MESH,
            )
            copy.start()
            sent.append(copy)
        for copy in sent:
            copy.wait()
        best = top
        for r in range(shards - 1):
            best = jnp.maximum(best, stats[r][:, 0:1])
        total = total * jnp.exp(top - best)
        for r in range(shards - 1):
            total = total + stats[r][:, 1:2] * jnp.exp(stats[r][:, 0:1] - best)
            picked = picked + stats[r][:, 2:3]
        lse = best + jnp.log(total)
        dsend[...] = jnp.broadcast_to(off[:, 0:1] - lse, dsend.shape)
        dcopies = []
        for r in range(1, owners):
            to = peer(r)
            copy = pltpu.make_async_remote_copy(
                src_ref=dsend.at[pl.ds(pl.multiple_of(to * slab, slab), slab), :],
                dst_ref=drecv.at[my_rows, :],
                send_sem=dssem.at[0],
                recv_sem=drsem.at[0],
                device_id=(to, mine),
                device_id_type=MESH,
            )
            copy.start()
        pltpu.make_async_copy(dsend.at[my_rows, :], drecv.at[my_rows, :], drsem.at[0]).start()
        target_ref[...] = jnp.transpose(
            jnp.broadcast_to(picked - lse, (tokens, LANES))
        )[0:1, :]

        row_k = lax.broadcasted_iota(jnp.int32, (kinds * slab, rows), 0)
        freqs = (row_k // slab + 1).astype(jnp.float32)
        at_steps = spread_steps(steps_ref, (kinds * slab, rows), slab)
        basis = jnp.cos(jnp.pi * freqs * at_steps / 143000.0)
        basis = basis - jnp.mean(basis, axis=1, keepdims=True)
        same = (row_k % slab) == (lax.broadcasted_iota(jnp.int32, (kinds * slab, rows), 1) % slab)
        keep = same & (row_k // slab < comps_ref[0])
        ones = jnp.ones((tile, LANES), jnp.bfloat16)

        def absorb(j, carry):
            products, totals = carry
            block = xrecv.at[:, columns(j)]
            pltpu.make_async_copy(block, block, recv_sem.at[j]).wait()
            pltpu.make_async_copy(block, xout_ref.at[:, columns(j)], out_sem.at[0]).start()
            x = block[...]
            products = products + lax.dot_general(x, x, NT, preferred_element_type=jnp.float32)
            totals = totals + jnp.dot(x, ones, preferred_element_type=jnp.float32)
            return products, totals

        products, totals = lax.fori_loop(
            0, chunks, absorb,
            (jnp.zeros((rows, rows), jnp.float32), jnp.zeros((rows, LANES), jnp.float32)),
        )
        pltpu.make_async_copy(drecv, drecv, drsem.at[0]).wait()
        d = drecv[...].reshape(owners, slab, LANES)
        d = (d - jnp.mean(d, axis=0, keepdims=True)).reshape(rows, LANES)
        lane_r = lax.broadcasted_iota(jnp.int32, (rows, LANES), 1)
        left = jnp.where(lane_r == 0, totals, jnp.where(lane_r == 1, d, 0.0))
        right = jnp.where(
            lane_r == 0, d, jnp.where(lane_r == 1, totals + float(width) * d, 0.0)
        )
        products = products + lax.dot_general(
            left, right, NT, precision=HIGH, preferred_element_type=jnp.float32
        )
        matched = (
            lax.broadcasted_iota(jnp.int32, (rows, rows), 0) % slab
            == lax.broadcasted_iota(jnp.int32, (rows, rows), 1) % slab
        )
        partial = jnp.sum(
            jnp.where(matched, products, 0.0).reshape(owners, slab, rows), axis=1
        )
        gsend[...] = partial
        gcopies = []
        for r in range(1, owners):
            copy = pltpu.make_async_remote_copy(
                src_ref=gsend,
                dst_ref=grecv.at[me],
                send_sem=gssem.at[0],
                recv_sem=grsem.at[0],
                device_id=(peer(r), mine),
                device_id_type=MESH,
            )
            copy.start()
        pltpu.make_async_copy(gsend, grecv.at[me], grsem.at[0]).start()
        pltpu.make_async_copy(grecv, grecv, grsem.at[0]).wait()
        hsend[...] = jnp.sum(grecv[...], axis=0)
        for r in range(1, shards):
            pltpu.make_async_remote_copy(
                src_ref=hsend,
                dst_ref=hrecv.at[mine],
                send_sem=hssem.at[0],
                recv_sem=hrsem.at[0],
                device_id=(me, side(r)),
                device_id_type=MESH,
            ).start()
        pltpu.make_async_copy(hsend, hrecv.at[mine], hrsem.at[0]).start()
        pltpu.make_async_copy(hrecv, hrecv, hrsem.at[0]).wait()
        full = jnp.sum(hrecv[...], axis=0) * (1.0 / (tokens * width * shards))
        full = full - jnp.mean(full, axis=0, keepdims=True)
        own = (
            lax.broadcasted_iota(jnp.int32, (owners, rows), 0)
            == lax.broadcasted_iota(jnp.int32, (owners, rows), 1) // slab
        )
        trace = jnp.sum(
            jnp.sum(jnp.where(own, full, 0.0), axis=1, keepdims=True), axis=0, keepdims=True
        )
        tall = jnp.broadcast_to(full[:, None, :], (owners, slab, rows)).reshape(rows, rows)
        mixed = lax.dot_general(
            basis, tall, NT, precision=HIGH, preferred_element_type=jnp.float32
        )
        mixed = jnp.where(keep, mixed / (trace * (1.0 / owners) + 1e-06) * (1.0 / owners), 0.0)
        high = mixed.astype(jnp.bfloat16)
        whi_ref[...] = high
        wlo_ref[...] = (mixed - high.astype(jnp.float32)).astype(jnp.bfloat16)
        shift_ref[...] = jnp.dot(mixed, d, precision=HIGH, preferred_element_type=jnp.float32)
        pick = (
            lax.broadcasted_iota(jnp.int32, (rows, LANES), 0) // slab
            == lax.broadcasted_iota(jnp.int32, (rows, LANES), 1)
        ).astype(jnp.float32) - 1.0 / owners
        gram_ref[...] = jnp.dot(
            full, pick, precision=HIGH, preferred_element_type=jnp.float32
        )[:, :owners]

        for r in range(1, owners):
            strip = xsend.at[my_rows, :]
            pltpu.make_async_copy(strip, strip, send_sem.at[r]).wait()
        others = pl.ds(0, rows - slab)
        pltpu.make_async_copy(dsend.at[others, :], dsend.at[others, :], dssem.at[0]).wait()
        less = pl.ds(0, owners - 1)
        pltpu.make_async_copy(grecv.at[less], grecv.at[less], gssem.at[0]).wait()
        fewer = pl.ds(0, shards - 1)
        pltpu.make_async_copy(hrecv.at[fewer], hrecv.at[fewer], hssem.at[0]).wait()
        pltpu.make_async_copy(xrecv, xout_ref, out_sem.at[0]).wait()


def mix_kernel(x_ref, whi_ref, wlo_ref, shift_ref, gram_in, target_in, out_ref, gram_ref, target_ref):
    x = x_ref[...]
    mixed = jnp.dot(whi_ref[...], x, preferred_element_type=jnp.float32)
    mixed = mixed + jnp.dot(wlo_ref[...], x, preferred_element_type=jnp.float32)
    out_ref[...] = (mixed + shift_ref[:, 0:1]).astype(jnp.bfloat16)
    gram_ref[...] = gram_in[...]
    target_ref[...] = target_in[...]


def per_device(owners, shards, hidden_rows, norm_gain, norm_bias, unembed, target_ids, ckpt_steps, components):
    tokens, depth = hidden_rows.shape[1:]
    width = unembed.shape[2]
    slab = tokens // owners
    rows = owners * slab
    out_rows = COMPONENTS * slab
    tile, chunks = split_tiles(width)
    padded = tile * chunks
    sizes = (owners, shards, tokens, width, tile, chunks)
    f32, bf16 = jnp.float32, jnp.bfloat16
    vmem = pl.BlockSpec(memory_space=pltpu.VMEM)
    smem = pl.BlockSpec(memory_space=pltpu.SMEM)
    dma = pltpu.SemaphoreType.DMA

    x, whi, wlo, shift, gram, target = pl.pallas_call(
        functools.partial(gather_kernel, sizes),
        grid=(chunks,),
        in_specs=[
            vmem, vmem, vmem, vmem, smem, smem,
            pl.BlockSpec((depth, tile), lambda j: (0, j)),
        ],
        out_specs=[pl.BlockSpec(memory_space=pl.ANY), vmem, vmem, vmem, vmem, vmem],
        out_shape=[
            jax.ShapeDtypeStruct((rows, padded), bf16),
            jax.ShapeDtypeStruct((out_rows, rows), bf16),
            jax.ShapeDtypeStruct((out_rows, rows), bf16),
            jax.ShapeDtypeStruct((out_rows, LANES), f32),
            jax.ShapeDtypeStruct((owners, owners), f32),
            jax.ShapeDtypeStruct((1, tokens), f32),
        ],
        scratch_shapes=[
            pltpu.VMEM((tokens, depth), bf16),
            pltpu.VMEM((tokens, padded), bf16),
            pltpu.VMEM((rows, padded), bf16),
            pltpu.VMEM((tokens, LANES), f32),
            pltpu.VMEM((tokens, LANES), jnp.int32),
            pltpu.VMEM((tokens, LANES), f32),
            pltpu.VMEM((tokens, LANES), f32),
            pltpu.VMEM((tokens, LANES), f32),
            pltpu.VMEM((tokens, LANES), f32),
            pltpu.VMEM((shards - 1, tokens, LANES), f32),
            pltpu.VMEM((tokens, LANES), f32),
            pltpu.VMEM((rows, LANES), f32),
            pltpu.VMEM((owners, rows), f32),
            pltpu.VMEM((owners, owners, rows), f32),
            pltpu.VMEM((owners, rows), f32),
            pltpu.VMEM((shards, owners, rows), f32),
            dma((owners,)), dma((chunks,)), dma((1,)),
            dma((shards - 1,)), dma((shards - 1,)),
            dma((1,)), dma((1,)), dma((1,)), dma((1,)), dma((1,)), dma((1,)),
        ],
        compiler_params=pltpu.CompilerParams(
            collective_id=0, has_side_effects=True, vmem_limit_bytes=60 * 1024 * 1024,
            dimension_semantics=("arbitrary",),
        ),
    )(
        hidden_rows[0], norm_gain, norm_bias, target_ids.reshape(1, tokens), ckpt_steps,
        components, unembed[0],
    )

    across = 3 * tile if chunks % 3 == 0 else tile
    out, gram, target = pl.pallas_call(
        mix_kernel,
        grid=(-(-padded // across),),
        in_specs=[pl.BlockSpec((rows, across), lambda j: (0, j)), vmem, vmem, vmem, vmem, vmem],
        out_specs=[pl.BlockSpec((out_rows, across), lambda j: (0, j)), vmem, vmem],
        out_shape=[
            jax.ShapeDtypeStruct((out_rows, width), bf16),
            jax.ShapeDtypeStruct((owners, owners), f32),
            jax.ShapeDtypeStruct((1, tokens), f32),
        ],
        compiler_params=pltpu.CompilerParams(dimension_semantics=("arbitrary",)),
    )(x, whi, wlo, shift, gram, target)
    return out.reshape(COMPONENTS, slab, width), gram, target


def solution(mesh):
    return jax.shard_map(
        functools.partial(per_device, mesh.shape["ckpt"], mesh.shape["vocab"]),
        mesh=mesh,
        in_specs=(
            P("ckpt", None, None),
            P("ckpt", None),
            P("ckpt", None),
            P("ckpt", None, "vocab"),
            P(),
            P(),
            P(),
        ),
        out_specs=(P(None, "ckpt", "vocab"), P(), P("ckpt", None)),
        check_vma=False,
    )
```

time: 188 us -> 88.6 us (0.47)
  Pallas kernels: 0 us -> 62.5 us
  blocking collectives: 61.7 us -> 0 us
  waiting for transfers between devices: 38.1 us -> 0 us
  matrix products: 35.3 us -> 0 us
  other arithmetic: 19.5 us -> 0 us
  starting transfers between devices: 3.84 us -> 0 us
  local copies, waits for them, and re-layouts: 26.8 us -> 23.8 us
    pallas_call x0 -> x2, Pallas kernels: none -> 62.5 us  [the longest x1 53.4 us: per_device(): pl.pallas_call(functools.partial(gather_kernel, sizes), grid=(chunks,), i...]
    psum x2 -> x0, blocking collectives: 48.2 us -> none  [the longest x1 39.9 us: per_device(): gram = lax.psum(partial_gram, ('ckpt', 'vocab')) / (tokens * width * shards)]
    all_to_all x1 -> x0, waiting for transfers between devices: 38.1 us -> none  [per_device(): lax.all_to_all(outgoing, 'ckpt', split_axis=1, concat_axis=0, tiled=True)]
    dot_general x4 -> x0, matrix products: 35.3 us -> none  [the longest x1 14.3 us: per_device(): partial_gram = jnp.dot(centred, centred.T, precision=lax.Precision.HIGHEST)]
    unnamed x7 -> x1, local copies, waits for them, and re-layouts: 6.47 us -> 23.8 us
    convert_element_type x3 -> x0, local copies, waits for them, and re-layouts: 17.1 us -> none  [the longest x1 7.04 us: per_device(): (mixed * keep[:, None]).reshape(kinds, slab, width).astype(jnp.bfloat16)]
    pmax x1 -> x0, blocking collectives: 13.5 us -> none  [normalize_rows(): top = lax.pmax(local_top, 'vocab')]
    reduce_sum x5 -> x0, other arithmetic: 12 us -> none  [the longest x1 8.76 us: normalize_rows(): target_logit = jnp.sum(jnp.where(hits, logits, 0.0), axis=1)]
  transfers between devices with their start and end apart: 1 -> 0, of which waited for: 1 -> 0; matrix products, arithmetic and copies ran while one was open for 0% -> 0% of each run, Pallas kernels for 0% -> 0%
where the time goes in v1:
time: 88.6 us; the launch traced here: 87.6 us
  Pallas kernels  62.5 us (71%)
  local copies, waits for them, and re-layouts  23.8 us (27%)
  between operations  1.29 us (1%)
    pallas_call x1, Pallas kernels, per_device(): pl.pallas_call(functools.partial(gather_kernel, sizes), grid=(chunks,), i...  53.4 us
    unnamed x1, local copies, waits for them, and re-layouts  23.8 us
    pallas_call x1, Pallas kernels, per_device(): pl.pallas_call(mix_kernel, grid=(-(-padded // across),), in_specs=[pl.Blo...  9.13 us

profile of v1, /device:TPU:0, one launch (start us, length us, event | category | flops | bytes accessed | tf_op | source)
XLA Modules:
  0.0 87.6 jit_solution(1537500087415590711)
XLA Ops:
  1.3 23.8 %copy.10 = bf16[1,768,12576]{2,1,0:T(8,128)(2,1)} copy(bf16[1,768,12576]{1,2,0:T(8,128)(2,1)} %param.10) | data formatting | bytes 38633472 | tf_op args[3]
  25.0 53.4 %shard_map.94 = (bf16[128,12672]{1,0:T(8,128)(2,1)}, bf16[128,128]{1,0:T(8,128)(2,1)}, bf16[128,128]{1,0:T(8,128)(2,1)}, f32[128,128]{1,0:T(8,128)}, f32[8,8]{1,0:T(8,128)}, /*index=5*/f32[1,128]{1,0:T(1,128)}) custom-call(bf16[128,768]{1,0:T(8,128)(2,1)} %bitcast.5, f32[1,768]{1,0:T(1,128)} %gain_ref.1, f32[1,768]{1,0:T(1,128)} %bias_ref.1, ...), custom_call_target="tpu_custom_call" | custom-call | tf_op jit(solution)/shard_map/pallas_call | solution.py:316
  78.4 9.1 %shard_map.95 = (bf16[128,12576]{1,0:T(8,128)(2,1)}, f32[8,8]{1,0:T(8,128)}, f32[1,128]{1,0:T(1,128)}) custom-call(bf16[128,12672]{1,0:T(8,128)(2,1)} %get-tuple-element.12.x_ref, bf16[128,128]{1,0:T(8,128)(2,1)} %get-tuple-element.13.whi_ref, bf16[128,128]{1,0:T(8,128)(2,1)} %get-tuple-element.14.wlo_ref, f32[128,128]{1,0:T(8,128)} %get-tuple-element.15.shift_ref, ...), custom_call_target="tpu_custom_call" | custom-call | tf_op jit(solution)/shard_map/pallas_call | solution.py:363

commit v2 on v1

--- a/solution.py
+++ b/solution.py
@@ -36,7 +36,7 @@
 def gather_kernel(
     sizes,
     hidden_ref, gain_ref, bias_ref, ids_ref, steps_ref, comps_ref, w_ref,
-    xout_ref, whi_ref, wlo_ref, shift_ref, gram_ref, target_ref,
+    xout_ref, w2_ref, shift_ref, gram_ref, target_ref,
     normed, xsend, xrecv, off, ids, tops, sums, hits, stat, stats, dsend, drecv,
     gsend, grecv, hsend, hrecv,
     send_sem, recv_sem, out_sem, ssend, srecv, dssem, drsem, gssem, grsem, hssem, hrsem,
@@ -76,7 +76,7 @@
         sums[...] = jnp.zeros_like(sums)
         hits[...] = jnp.zeros_like(hits)
 
-    logits = jnp.dot(normed[...], w_ref[...], preferred_element_type=jnp.float32)
+    logits = lax.dot_general(normed[...], w_ref[...], NT, preferred_element_type=jnp.float32)
     first = step * tile
     lane = lax.broadcasted_iota(jnp.int32, (tokens, LANES), 1)
 
@@ -267,8 +267,9 @@
         )
         mixed = jnp.where(keep, mixed / (trace * (1.0 / owners) + 1e-06) * (1.0 / owners), 0.0)
         high = mixed.astype(jnp.bfloat16)
-        whi_ref[...] = high
-        wlo_ref[...] = (mixed - high.astype(jnp.float32)).astype(jnp.bfloat16)
+        half = mixed.shape[0]
+        w2_ref[0:half, :] = high
+        w2_ref[half:, :] = (mixed - high.astype(jnp.float32)).astype(jnp.bfloat16)
         shift_ref[...] = jnp.dot(mixed, d, precision=HIGH, preferred_element_type=jnp.float32)
         pick = (
             lax.broadcasted_iota(jnp.int32, (rows, LANES), 0) // slab
@@ -290,11 +291,12 @@
         pltpu.make_async_copy(xrecv, xout_ref, out_sem.at[0]).wait()
 
 
-def mix_kernel(x_ref, whi_ref, wlo_ref, shift_ref, gram_in, target_in, out_ref, gram_ref, target_ref):
-    x = x_ref[...]
-    mixed = jnp.dot(whi_ref[...], x, preferred_element_type=jnp.float32)
-    mixed = mixed + jnp.dot(wlo_ref[...], x, preferred_element_type=jnp.float32)
-    out_ref[...] = (mixed + shift_ref[:, 0:1]).astype(jnp.bfloat16)
+def mix_kernel(across, x_ref, w2_ref, shift_ref, gram_in, target_in, out_ref, gram_ref, target_ref):
+    start = pl.multiple_of(pl.program_id(0) * across, LANES)
+    x = x_ref[:, pl.ds(start, across)]
+    both = jnp.dot(w2_ref[...], x, preferred_element_type=jnp.float32)
+    half = out_ref.shape[0]
+    out_ref[...] = (both[:half] + both[half:] + shift_ref[:, 0:1]).astype(jnp.bfloat16)
     gram_ref[...] = gram_in[...]
     target_ref[...] = target_in[...]
 
@@ -309,22 +311,22 @@
     padded = tile * chunks
     sizes = (owners, shards, tokens, width, tile, chunks)
     f32, bf16 = jnp.float32, jnp.bfloat16
+    limit = 67043328 - rows * padded * 2 - (5 << 19)
     vmem = pl.BlockSpec(memory_space=pltpu.VMEM)
     smem = pl.BlockSpec(memory_space=pltpu.SMEM)
     dma = pltpu.SemaphoreType.DMA
 
-    x, whi, wlo, shift, gram, target = pl.pallas_call(
+    x, w2, shift, gram, target = pl.pallas_call(
         functools.partial(gather_kernel, sizes),
         grid=(chunks,),
         in_specs=[
             vmem, vmem, vmem, vmem, smem, smem,
-            pl.BlockSpec((depth, tile), lambda j: (0, j)),
+            pl.BlockSpec((tile, depth), lambda j: (j, 0)),
         ],
-        out_specs=[pl.BlockSpec(memory_space=pl.ANY), vmem, vmem, vmem, vmem, vmem],
+        out_specs=[pl.BlockSpec(memory_space=pl.ANY), vmem, vmem, vmem, vmem],
         out_shape=[
             jax.ShapeDtypeStruct((rows, padded), bf16),
-            jax.ShapeDtypeStruct((out_rows, rows), bf16),
-            jax.ShapeDtypeStruct((out_rows, rows), bf16),
+            jax.ShapeDtypeStruct((2 * out_rows, rows), bf16),
             jax.ShapeDtypeStruct((out_rows, LANES), f32),
             jax.ShapeDtypeStruct((owners, owners), f32),
             jax.ShapeDtypeStruct((1, tokens), f32),
@@ -351,27 +353,30 @@
             dma((1,)), dma((1,)), dma((1,)), dma((1,)), dma((1,)), dma((1,)),
         ],
         compiler_params=pltpu.CompilerParams(
-            collective_id=0, has_side_effects=True, vmem_limit_bytes=60 * 1024 * 1024,
+            collective_id=0, has_side_effects=True, vmem_limit_bytes=limit,
             dimension_semantics=("arbitrary",),
         ),
     )(
         hidden_rows[0], norm_gain, norm_bias, target_ids.reshape(1, tokens), ckpt_steps,
-        components, unembed[0],
+        components, unembed[0].T,
     )
 
-    across = 3 * tile if chunks % 3 == 0 else tile
+    across = -(-(padded // LANES) // 3) * LANES
     out, gram, target = pl.pallas_call(
-        mix_kernel,
-        grid=(-(-padded // across),),
-        in_specs=[pl.BlockSpec((rows, across), lambda j: (0, j)), vmem, vmem, vmem, vmem, vmem],
+        functools.partial(mix_kernel, across),
+        grid=(padded // across,),
+        in_specs=[vmem, vmem, vmem, vmem, vmem],
         out_specs=[pl.BlockSpec((out_rows, across), lambda j: (0, j)), vmem, vmem],
         out_shape=[
             jax.ShapeDtypeStruct((out_rows, width), bf16),
             jax.ShapeDtypeStruct((owners, owners), f32),
             jax.ShapeDtypeStruct((1, tokens), f32),
         ],
-        compiler_params=pltpu.CompilerParams(dimension_semantics=("arbitrary",)),
-    )(x, whi, wlo, shift, gram, target)
+        compiler_params=pltpu.CompilerParams(
+            dimension_semantics=("arbitrary",),
+            vmem_limit_bytes=rows * padded * 2 + 12 * out_rows * across + (6 << 20),
+        ),
+    )(x, w2, shift, gram, target)
     return out.reshape(COMPONENTS, slab, width), gram, target
 
 

time: 88.6 us -> 63.6 us (0.72)
  local copies, waits for them, and re-layouts: 23.8 us -> 4.94 us
  Pallas kernels: 62.5 us -> 56.9 us
    unnamed x1 -> x10, local copies, waits for them, and re-layouts: 23.8 us -> 4.94 us
    pallas_call x1, Pallas kernels: 9.13 us -> 3.41 us  [per_device(): pl.pallas_call(functools.partial(mix_kernel, across), grid=(padded // acr...]
where the time goes in v2:
time: 63.6 us; the launch traced here: 63.1 us
  Pallas kernels  56.9 us (89%)
  local copies, waits for them, and re-layouts  4.94 us (8%)
  between operations  1.3 us (2%)
    pallas_call x1, Pallas kernels, per_device(): pl.pallas_call(functools.partial(gather_kernel, sizes), grid=(chunks,), i...  53.4 us
    unnamed x10, local copies, waits for them, and re-layouts  4.94 us
    pallas_call x1, Pallas kernels, per_device(): pl.pallas_call(functools.partial(mix_kernel, across), grid=(padded // acr...  3.41 us

profile of v2, /device:TPU:0, one launch (start us, length us, event | category | flops | bytes accessed | tf_op | source)
XLA Modules:
  0.0 63.1 jit_solution(15065823453593846627)
XLA Ops:
  1.3 53.4 %shard_map.94 = (bf16[128,12672]{1,0:T(8,128)(2,1)}, bf16[256,128]{1,0:T(8,128)(2,1)}, f32[128,128]{1,0:T(8,128)}, f32[8,8]{1,0:T(8,128)}, f32[1,128]{1,0:T(1,128)}) custom-call(bf16[128,768]{1,0:T(8,128)(2,1)} %bitcast.7, f32[1,768]{1,0:T(1,128)} %gain_ref.1, f32[1,768]{1,0:T(1,128)} %bias_ref.1, s32[1,128]{1,0:T(1,128)} %bitcast.8, s32[8]{0:T(128)} %steps_ref.1, ...), custom_call_target="tpu_custom_call" | custom-call | tf_op jit(solution)/shard_map/pallas_call | solution.py:319
  54.7 0.0 copy-start
  54.7 1.9 %copy-done = bf16[128,12672]{1,0:T(8,128)(2,1)S(1)} copy-done((bf16[128,12672]{1,0:T(8,128)(2,1)S(1)}, bf16[128,12672]{1,0:T(8,128)(2,1)}, u32[]{:S(2)}) %copy-start) | copy-done | bytes 3244056
  56.6 0.0 copy-start.1
  56.6 0.8 %copy-done.1 = bf16[256,128]{1,0:T(8,128)(2,1)S(1)} copy-done((bf16[256,128]{1,0:T(8,128)(2,1)S(1)}, bf16[256,128]{1,0:T(8,128)(2,1)}, u32[]{:S(2)}) %copy-start.1) | copy-done | bytes 65560
  57.5 0.0 copy-start.2
  57.5 0.8 %copy-done.2 = f32[128,128]{1,0:T(8,128)S(1)} copy-done((f32[128,128]{1,0:T(8,128)S(1)}, f32[128,128]{1,0:T(8,128)}, u32[]{:S(2)}) %copy-start.2) | copy-done | bytes 65560
  58.3 0.0 copy-start.3
  58.3 0.7 %copy-done.3 = f32[8,8]{1,0:T(8,128)S(1)} copy-done((f32[8,8]{1,0:T(8,128)S(1)}, f32[8,8]{1,0:T(8,128)}, u32[]{:S(2)}) %copy-start.3) | copy-done | bytes 280
  59.0 0.0 copy-start.4
  59.0 0.7 %copy-done.4 = f32[1,128]{1,0:T(1,128)S(1)} copy-done((f32[1,128]{1,0:T(1,128)S(1)}, f32[1,128]{1,0:T(1,128)}, u32[]{:S(2)}) %copy-start.4) | copy-done | bytes 536
  59.7 3.4 %shard_map.95 = (bf16[128,12576]{1,0:T(8,128)(2,1)}, f32[8,8]{1,0:T(8,128)}, f32[1,128]{1,0:T(1,128)}) custom-call(bf16[128,12672]{1,0:T(8,128)(2,1)S(1)} %copy-done, bf16[256,128]{1,0:T(8,128)(2,1)S(1)} %copy-done.1, f32[128,128]{1,0:T(8,128)S(1)} %copy-done.2, f32[8,8]{1,0:T(8,128)S(1)} %copy-done.3, f32[1,128]{1,0:T(1,128)S(1)} %copy-done.4), custom_call_target="tpu_custom_call" | custom-call | tf_op jit(solution)/shard_map/pallas_call | solution.py:365
Async XLA Ops:
  54.7 1.9 %copy-start = (bf16[128,12672]{1,0:T(8,128)(2,1)S(1)}, bf16[128,12672]{1,0:T(8,128)(2,1)}, u32[]{:S(2)}) copy-start(bf16[128,12672]{1,0:T(8,128)(2,1)} %get-tuple-element.11.x_ref) | copy-start | bytes 9732100
  56.6 0.8 %copy-start.1 = (bf16[256,128]{1,0:T(8,128)(2,1)S(1)}, bf16[256,128]{1,0:T(8,128)(2,1)}, u32[]{:S(2)}) copy-start(bf16[256,128]{1,0:T(8,128)(2,1)} %get-tuple-element.12.w2_ref) | copy-start | bytes 196612
  57.5 0.8 %copy-start.2 = (f32[128,128]{1,0:T(8,128)S(1)}, f32[128,128]{1,0:T(8,128)}, u32[]{:S(2)}) copy-start(f32[128,128]{1,0:T(8,128)} %get-tuple-element.13.shift_ref) | copy-start | bytes 196612
  58.3 0.7 %copy-start.3 = (f32[8,8]{1,0:T(8,128)S(1)}, f32[8,8]{1,0:T(8,128)}, u32[]{:S(2)}) copy-start(f32[8,8]{1,0:T(8,128)} %get-tuple-element.14.gram_in) | copy-start | bytes 772
  59.0 0.7 %copy-start.4 = (f32[1,128]{1,0:T(1,128)S(1)}, f32[1,128]{1,0:T(1,128)}, u32[]{:S(2)}) copy-start(f32[1,128]{1,0:T(1,128)} %get-tuple-element.15.target_in) | copy-start | bytes 1540

commit v3 on v2

--- a/solution.py
+++ b/solution.py
@@ -25,8 +25,8 @@
     return best * LANES, tiles // best
 
 
-def spread_steps(steps_ref, shape, slab):
-    lane_owner = lax.broadcasted_iota(jnp.int32, shape, 1) // slab
+def spread_steps(steps_ref, shape):
+    lane_owner = lax.broadcasted_iota(jnp.int32, shape, 1) % steps_ref.shape[0]
     out = jnp.zeros(shape, jnp.float32)
     for c in range(steps_ref.shape[0]):
         out = jnp.where(lane_owner == c, steps_ref[c].astype(jnp.float32), out)
@@ -35,11 +35,12 @@
 
 def gather_kernel(
     sizes,
-    hidden_ref, gain_ref, bias_ref, ids_ref, steps_ref, comps_ref, w_ref,
+    hidden_hbm, gain_hbm, bias_hbm, ids_hbm, steps_hbm, comps_hbm, w_ref,
     xout_ref, w2_ref, shift_ref, gram_ref, target_ref,
     normed, xsend, xrecv, off, ids, tops, sums, hits, stat, stats, dsend, drecv,
-    gsend, grecv, hsend, hrecv,
-    send_sem, recv_sem, out_sem, ssend, srecv, dssem, drsem, gssem, grsem, hssem, hrsem,
+    gsend, grecv,
+    hidden_ref, gain_ref, bias_ref, ids_ref, steps_ref, comps_ref, in_sem,
+    send_sem, recv_sem, out_sem, ssend, srecv, dssem, drsem, gssem, grsem,
 ):
     owners, shards, tokens, width, tile, chunks = sizes
     slab = tokens // owners
@@ -59,11 +60,23 @@
 
     @pl.when(step == 0)
     def _():
+        loads = []
+        for i, (src, dst) in enumerate((
+            (hidden_hbm, hidden_ref), (gain_hbm, gain_ref), (bias_hbm, bias_ref),
+            (ids_hbm, ids_ref), (steps_hbm, steps_ref), (comps_hbm, comps_ref),
+        )):
+            load = pltpu.make_async_copy(src, dst, in_sem.at[i])
+            load.start()
+            loads.append(load)
         barrier = pltpu.get_barrier_semaphore()
-        for r in range(1, owners):
-            pl.semaphore_signal(barrier, inc=1, device_id=(peer(r), mine), device_id_type=MESH)
-        for r in range(1, shards):
-            pl.semaphore_signal(barrier, inc=1, device_id=(me, side(r)), device_id_type=MESH)
+        for q in range(shards):
+            for r in range(owners):
+                if q or r:
+                    pl.semaphore_signal(
+                        barrier, inc=1, device_id=(peer(r), side(q)), device_id_type=MESH
+                    )
+        for load in loads:
+            load.wait()
         floats = hidden_ref[...].astype(jnp.float32)
         centre = jnp.mean(floats, axis=1, keepdims=True)
         spread = jnp.mean((floats - centre) ** 2, axis=1, keepdims=True)
@@ -99,7 +112,7 @@
     @pl.when(step == 0)
     def _():
         barrier = pltpu.get_barrier_semaphore()
-        pl.semaphore_wait(barrier, owners - 1 + shards - 1)
+        pl.semaphore_wait(barrier, owners * shards - 1)
 
     def columns(j):
         return pl.ds(pl.multiple_of(j * tile, LANES), tile)
@@ -185,13 +198,31 @@
             jnp.broadcast_to(picked - lse, (tokens, LANES))
         )[0:1, :]
 
-        row_k = lax.broadcasted_iota(jnp.int32, (kinds * slab, rows), 0)
-        freqs = (row_k // slab + 1).astype(jnp.float32)
-        at_steps = spread_steps(steps_ref, (kinds * slab, rows), slab)
-        basis = jnp.cos(jnp.pi * freqs * at_steps / 143000.0)
-        basis = basis - jnp.mean(basis, axis=1, keepdims=True)
-        same = (row_k % slab) == (lax.broadcasted_iota(jnp.int32, (kinds * slab, rows), 1) % slab)
-        keep = same & (row_k // slab < comps_ref[0])
+        flats = max(owners * owners, LANES)
+
+        def iota(shape, axis):
+            return lax.broadcasted_iota(jnp.int32, shape, axis)
+
+        slot = mine * owners + me
+        flat_lane = iota((owners, flats), 1)
+        flat_own = flat_lane // owners == iota((owners, flats), 0)
+        flat_diag = iota((1, flats), 1) // owners == iota((1, flats), 1) % owners
+        to_flat = (iota((rows, flats), 0) // slab == iota((rows, flats), 1) % owners).astype(
+            jnp.float32
+        )
+        from_flat = (iota((flats, rows), 0) // owners == iota((flats, rows), 1) // slab).astype(
+            jnp.float32
+        )
+        flat_pick = (iota((flats, LANES), 0) % owners == iota((flats, LANES), 1)).astype(
+            jnp.float32
+        ) - 1.0 / owners
+        row_k = iota((kinds * slab, flats), 0) // slab
+        at_steps = spread_steps(steps_ref, (kinds * slab, flats))
+        basis = jnp.cos(jnp.pi * (row_k + 1).astype(jnp.float32) * at_steps / 143000.0)
+        flat_basis = basis - jnp.mean(basis, axis=1, keepdims=True)
+        row_r = iota((kinds * slab, rows), 0)
+        same = (row_r % slab) == (iota((kinds * slab, rows), 1) % slab)
+        keep = same & (row_r // slab < comps_ref[0])
         ones = jnp.ones((tile, LANES), jnp.bfloat16)
 
         def absorb(j, carry):
@@ -211,6 +242,7 @@
         pltpu.make_async_copy(drecv, drecv, drsem.at[0]).wait()
         d = drecv[...].reshape(owners, slab, LANES)
         d = (d - jnp.mean(d, axis=0, keepdims=True)).reshape(rows, LANES)
+        d_row = jnp.transpose(d)[0:1, :]
         lane_r = lax.broadcasted_iota(jnp.int32, (rows, LANES), 1)
         left = jnp.where(lane_r == 0, totals, jnp.where(lane_r == 1, d, 0.0))
         right = jnp.where(
@@ -226,57 +258,38 @@
         partial = jnp.sum(
             jnp.where(matched, products, 0.0).reshape(owners, slab, rows), axis=1
         )
-        gsend[...] = partial
-        gcopies = []
-        for r in range(1, owners):
-            copy = pltpu.make_async_remote_copy(
-                src_ref=gsend,
-                dst_ref=grecv.at[me],
-                send_sem=gssem.at[0],
-                recv_sem=grsem.at[0],
-                device_id=(peer(r), mine),
-                device_id_type=MESH,
-            )
-            copy.start()
-        pltpu.make_async_copy(gsend, grecv.at[me], grsem.at[0]).start()
+        partial = partial - jnp.mean(partial, axis=0, keepdims=True)
+        spreadout = jnp.dot(partial, to_flat, precision=HIGH, preferred_element_type=jnp.float32)
+        gsend[...] = jnp.sum(jnp.where(flat_own, spreadout, 0.0), axis=0, keepdims=True)
+        for q in range(shards):
+            for r in range(owners):
+                if q or r:
+                    pltpu.make_async_remote_copy(
+                        src_ref=gsend,
+                        dst_ref=grecv.at[slot],
+                        send_sem=gssem.at[0],
+                        recv_sem=grsem.at[0],
+                        device_id=(peer(r), side(q)),
+                        device_id_type=MESH,
+                    ).start()
+        pltpu.make_async_copy(gsend, grecv.at[slot], grsem.at[0]).start()
         pltpu.make_async_copy(grecv, grecv, grsem.at[0]).wait()
-        hsend[...] = jnp.sum(grecv[...], axis=0)
-        for r in range(1, shards):
-            pltpu.make_async_remote_copy(
-                src_ref=hsend,
-                dst_ref=hrecv.at[mine],
-                send_sem=hssem.at[0],
-                recv_sem=hrsem.at[0],
-                device_id=(me, side(r)),
-                device_id_type=MESH,
-            ).start()
-        pltpu.make_async_copy(hsend, hrecv.at[mine], hrsem.at[0]).start()
-        pltpu.make_async_copy(hrecv, hrecv, hrsem.at[0]).wait()
-        full = jnp.sum(hrecv[...], axis=0) * (1.0 / (tokens * width * shards))
-        full = full - jnp.mean(full, axis=0, keepdims=True)
-        own = (
-            lax.broadcasted_iota(jnp.int32, (owners, rows), 0)
-            == lax.broadcasted_iota(jnp.int32, (owners, rows), 1) // slab
-        )
-        trace = jnp.sum(
-            jnp.sum(jnp.where(own, full, 0.0), axis=1, keepdims=True), axis=0, keepdims=True
-        )
-        tall = jnp.broadcast_to(full[:, None, :], (owners, slab, rows)).reshape(rows, rows)
-        mixed = lax.dot_general(
-            basis, tall, NT, precision=HIGH, preferred_element_type=jnp.float32
+        flat = jnp.sum(grecv[...], axis=0) * (1.0 / (tokens * width * shards))
+        trace = jnp.sum(jnp.where(flat_diag, flat, 0.0), axis=1, keepdims=True)
+        mixed = jnp.dot(
+            flat_basis * flat, from_flat, precision=HIGH, preferred_element_type=jnp.float32
         )
         mixed = jnp.where(keep, mixed / (trace * (1.0 / owners) + 1e-06) * (1.0 / owners), 0.0)
         high = mixed.astype(jnp.bfloat16)
         half = mixed.shape[0]
         w2_ref[0:half, :] = high
         w2_ref[half:, :] = (mixed - high.astype(jnp.float32)).astype(jnp.bfloat16)
-        shift_ref[...] = jnp.dot(mixed, d, precision=HIGH, preferred_element_type=jnp.float32)
-        pick = (
-            lax.broadcasted_iota(jnp.int32, (rows, LANES), 0) // slab
-            == lax.broadcasted_iota(jnp.int32, (rows, LANES), 1)
-        ).astype(jnp.float32) - 1.0 / owners
+        shift_ref[...] = jnp.broadcast_to(
+            jnp.sum(mixed * d_row, axis=1, keepdims=True), shift_ref.shape
+        )
         gram_ref[...] = jnp.dot(
-            full, pick, precision=HIGH, preferred_element_type=jnp.float32
+            jnp.where(flat_own, flat, 0.0), flat_pick, precision=HIGH,
+            preferred_element_type=jnp.float32,
         )[:, :owners]
 
         for r in range(1, owners):
@@ -284,10 +297,8 @@
             pltpu.make_async_copy(strip, strip, send_sem.at[r]).wait()
         others = pl.ds(0, rows - slab)
         pltpu.make_async_copy(dsend.at[others, :], dsend.at[others, :], dssem.at[0]).wait()
-        less = pl.ds(0, owners - 1)
+        less = pl.ds(0, owners * shards - 1)
         pltpu.make_async_copy(grecv.at[less], grecv.at[less], gssem.at[0]).wait()
-        fewer = pl.ds(0, shards - 1)
-        pltpu.make_async_copy(hrecv.at[fewer], hrecv.at[fewer], hssem.at[0]).wait()
         pltpu.make_async_copy(xrecv, xout_ref, out_sem.at[0]).wait()
 
 
@@ -311,16 +322,16 @@
     padded = tile * chunks
     sizes = (owners, shards, tokens, width, tile, chunks)
     f32, bf16 = jnp.float32, jnp.bfloat16
-    limit = 67043328 - rows * padded * 2 - (5 << 19)
+    limit = 67043328 - min(depth * width * 2 - (1 << 20), 16 << 20)
     vmem = pl.BlockSpec(memory_space=pltpu.VMEM)
-    smem = pl.BlockSpec(memory_space=pltpu.SMEM)
+    hbm = pl.BlockSpec(memory_space=pltpu.HBM)
     dma = pltpu.SemaphoreType.DMA
 
     x, w2, shift, gram, target = pl.pallas_call(
         functools.partial(gather_kernel, sizes),
         grid=(chunks,),
         in_specs=[
-            vmem, vmem, vmem, vmem, smem, smem,
+            hbm, hbm, hbm, hbm, hbm, hbm,
             pl.BlockSpec((tile, depth), lambda j: (j, 0)),
         ],
         out_specs=[pl.BlockSpec(memory_space=pl.ANY), vmem, vmem, vmem, vmem],
@@ -344,22 +355,28 @@
             pltpu.VMEM((shards - 1, tokens, LANES), f32),
             pltpu.VMEM((tokens, LANES), f32),
             pltpu.VMEM((rows, LANES), f32),
-            pltpu.VMEM((owners, rows), f32),
-            pltpu.VMEM((owners, owners, rows), f32),
-            pltpu.VMEM((owners, rows), f32),
-            pltpu.VMEM((shards, owners, rows), f32),
+            pltpu.VMEM((1, max(owners * owners, LANES)), f32),
+            pltpu.VMEM((owners * shards, 1, max(owners * owners, LANES)), f32),
+            pltpu.VMEM((tokens, depth), bf16),
+            pltpu.VMEM((1, depth), f32),
+            pltpu.VMEM((1, depth), f32),
+            pltpu.VMEM((1, tokens), jnp.int32),
+            pltpu.SMEM((owners,), jnp.int32),
+            pltpu.SMEM((1,), jnp.int32),
+            dma((6,)),
             dma((owners,)), dma((chunks,)), dma((1,)),
             dma((shards - 1,)), dma((shards - 1,)),
-            dma((1,)), dma((1,)), dma((1,)), dma((1,)), dma((1,)), dma((1,)),
+            dma((1,)), dma((1,)), dma((1,)), dma((1,)),
         ],
         compiler_params=pltpu.CompilerParams(
             collective_id=0, has_side_effects=True, vmem_limit_bytes=limit,
             dimension_semantics=("arbitrary",),
         ),
-    )(
-        hidden_rows[0], norm_gain, norm_bias, target_ids.reshape(1, tokens), ckpt_steps,
-        components, unembed[0].T,
-    )
+    )(*(
+        pltpu.with_memory_space_constraint(a, pltpu.HBM) for a in (
+            hidden_rows[0], norm_gain, norm_bias, target_ids.reshape(1, tokens), ckpt_steps,
+        )
+    ), components, unembed[0].T)
 
     across = -(-(padded // LANES) // 3) * LANES
     out, gram, target = pl.pallas_call(

time: 63.6 us -> 55.8 us (0.88)
  local copies, waits for them, and re-layouts: 4.94 us -> 0 us
  Pallas kernels: 56.9 us -> 54.1 us
    unnamed x10 -> x0, local copies, waits for them, and re-layouts: 4.94 us -> none
    pallas_call x1, Pallas kernels: 53.4 us -> 50.7 us  [per_device(): pl.pallas_call(functools.partial(gather_kernel, sizes), grid=(chunks,), i...]
where the time goes in v3:
time: 55.8 us; the launch traced here: 55.4 us
  Pallas kernels  54.1 us (97%)
  between operations  1.29 us (2%)
    pallas_call x1, Pallas kernels, per_device(): pl.pallas_call(functools.partial(gather_kernel, sizes), grid=(chunks,), i...  50.7 us
    pallas_call x1, Pallas kernels, per_device(): pl.pallas_call(functools.partial(mix_kernel, across), grid=(padded // acr...  3.43 us

profile of v3, /device:TPU:0, one launch (start us, length us, event | category | flops | bytes accessed | tf_op | source)
XLA Modules:
  0.0 55.4 jit_solution(17574855789525596128)
XLA Ops:
  1.3 50.7 %shard_map.94 = (bf16[128,12672]{1,0:T(8,128)(2,1)S(1)}, bf16[256,128]{1,0:T(8,128)(2,1)S(1)}, f32[128,128]{1,0:T(8,128)S(1)}, f32[8,8]{1,0:T(8,128)S(1)}, f32[1,128]{1,0:T(1,128)S(1)}) custom-call(bf16[128,768]{1,0:T(8,128)(2,1)} %bitcast.7, f32[1,768]{1,0:T(1,128)} %gain_hbm.1, f32[1,768]{1,0:T(1,128)} %bias_hbm.1, s32[1,128]{1,0:T(1,128)} %bitcast.8, ...), custom_call_target="tpu_custom_call" | custom-call | tf_op jit(solution)/shard_map/pallas_call | solution.py:330
  52.0 3.4 %shard_map.95 = (bf16[128,12576]{1,0:T(8,128)(2,1)}, f32[8,8]{1,0:T(8,128)}, f32[1,128]{1,0:T(1,128)}) custom-call(bf16[128,12672]{1,0:T(8,128)(2,1)S(1)} %get-tuple-element.11.x_ref, bf16[256,128]{1,0:T(8,128)(2,1)S(1)} %get-tuple-element.12.w2_ref, f32[128,128]{1,0:T(8,128)S(1)} %get-tuple-element.13.shift_ref, f32[8,8]{1,0:T(8,128)S(1)} %get-tuple-element.14.gram_in, ...), custom_call_target="tpu_custom_call" | custom-call | tf_op jit(solution)/shard_map/pallas_call | solution.py:382
